TPU v7x, 256 devices: a whole 4x4x8 slice. The times are simulated.
256 devices in a mesh: seq: 16 (over y, x), exp: 16 (over z, core).
Axes of the slice: x: 4, y: 4, z: 8, core: 2. Of those that a mesh axis runs over, the one named last changes fastest.
Arguments:
- x_in: bfloat16 [4096, 8192], P('seq', 'exp'), may hold values from -6 to 6
- z_gate: bfloat16 [4096, 8192], P('seq', 'exp'), may hold values from -6 to 6
- b_in: bfloat16 [4096, 128], P('seq'), may hold values from -0.52734375 to 0.52734375
- c_out: bfloat16 [4096, 128], P('seq'), may hold values from -0.1875 to 0.1875
- dt_step: float32 [4096, 128], P('seq', 'exp'), may hold values from 0.12 to 2052, as said below
- rate: float32 [128], P('exp'), may hold values from 0 to 0.06, as said below
- skip: float32 [128], P('exp'), may hold values from 0.5 to 1.5
- init_state: float32 [128, 64, 128], P('exp'), may hold values from -16.970562 to 16.970562
- residual: bfloat16 [4096, 8192], P(('seq', 'exp')), may hold values from -6 to 6
- norm_gain: float32 [8192], replicated, may hold values from 0.5 to 1.5
- expert_ids: int32 [4096, 2], P(('seq', 'exp')), may hold values from 0 to 15, all different within a row; in each aligned block of 16 rows (0 to 15, 16 to 31, ...) at most 3 rows name the same one
- gate_weights: float32 [4096, 2], P(('seq', 'exp')), may hold values from 0.2 to 1
- w_gate: bfloat16 [16, 8192, 2048], P('exp', None, 'seq'), may hold values from -0.0625 to 0.0625
- w_up: bfloat16 [16, 8192, 2048], P('exp', None, 'seq'), may hold values from -0.0625 to 0.0625
- w_down: bfloat16 [16, 2048, 8192], P('exp', 'seq'), may hold values from -0.125 to 0.125
Outputs:
- layer_out: bfloat16 [4096, 8192], P(('seq', 'exp'))
Inputs may be any that keep to these rules, and one draw needn't show every extreme that they name: `dt_step`: positive step sizes. `rate`: positive rates. `expert_ids`: each row names two different experts; among the rows of one device (aligned blocks of 16 rows) no expert is named by more than 3 rows, and in every draw some expert is named by exactly 3 rows of some block.
All inputs are finite; a program needn't handle non-finite values.
Results may differ from a plain program's by a relative error of at most 0.0095.
Values may be sent and summed in bfloat16 or wider, within the bound.
A program may use at most 128 MiB of HBM per device.

v0:
```python
import jax
import jax.numpy as jnp
from jax import lax
from jax.sharding import PartitionSpec as P

GROUP = 128
PRECISE = lax.Precision.HIGHEST


def entering_2(array, axis, combine, identity):
    devices, mine = (lax.axis_size(axis), lax.axis_index(axis))
    everything = jax.tree.map(
        lambda part, kind: lax.all_gather(part.astype(kind), axis),
        array,
        (jnp.bfloat16, jnp.bfloat16),
    )
    start = jax.tree.map(
        lambda part, zero: jnp.broadcast_to(jnp.asarray(zero, part.dtype), part.shape),
        array,
        identity,
    )

    def hop(k, before):
        reached = k < mine
        new = combine(
            before, jax.tree.map(lambda part, own: part[k].astype(own.dtype), everything, array)
        )
        return jax.tree.map(lambda a, b: jnp.where(reached, a, b), new, before)

    return lax.fori_loop(0, devices, hop, start)


def chain_combine(earlier, later):
    return (earlier[0] + later[0], jnp.exp(later[0])[:, None, None] * earlier[1] + later[1])


def on_device(
    x_in,
    z_gate,
    b_in,
    c_out,
    dt_step,
    rate,
    skip,
    init_state,
    residual,
    norm_gain,
    expert_ids,
    gate_weights,
    w_gate,
    w_up,
    w_down,
):
    token_count, channels = x_in.shape
    heads_here = rate.shape[0]
    head_width = channels // heads_here
    state_width = b_in.shape[1]
    blocks = token_count // GROUP
    inputs = x_in.astype(jnp.float32).reshape(blocks, GROUP, heads_here, head_width)
    keys_in = b_in.astype(jnp.float32).reshape(blocks, GROUP, state_width)
    queries = c_out.astype(jnp.float32).reshape(blocks, GROUP, state_width)
    log_steps = (-rate[None, :] * dt_step).reshape(blocks, GROUP, heads_here)
    cumulative = jnp.cumsum(log_steps, axis=1)
    scores = jnp.einsum("ctn,csn->cts", queries, keys_in, precision=PRECISE)
    causal = jnp.arange(GROUP)[:, None] >= jnp.arange(GROUP)[None, :]
    spread = cumulative[:, :, None, :] - cumulative[:, None, :, :]
    weights = jnp.exp(jnp.where(causal[None, :, :, None], spread, -jnp.inf)) * scores[..., None]
    intra_out = jnp.einsum("ctsh,cshp->cthp", weights, inputs, precision=PRECISE)
    tail_decay = jnp.exp(cumulative[:, -1:, :] - cumulative)
    block_state = jnp.einsum("csh,cshp,csn->chpn", tail_decay, inputs, keys_in, precision=PRECISE)
    block_log = cumulative[:, -1, :]

    def advance(carried, element):
        total_log, total_state = carried
        step_log, step_state = element
        updated = (
            total_log + step_log,
            jnp.exp(step_log)[:, None, None] * total_state + step_state,
        )
        return (updated, (total_log, total_state))

    zero_state = jnp.zeros((heads_here, head_width, state_width), jnp.float32)
    zero_log = jnp.zeros((heads_here,), jnp.float32)
    (device_log, device_state), (enter_log, enter_state) = lax.scan(
        advance, (zero_log, zero_state), (block_log, block_state)
    )
    prior_log, prior_state = entering_2(
        (device_log, device_state), "seq", chain_combine, (zero_log, zero_state)
    )
    incoming = prior_state + jnp.exp(prior_log)[:, None, None] * init_state
    entering = enter_state + jnp.exp(enter_log)[:, :, None, None] * incoming[None]
    inter_out = jnp.exp(cumulative)[..., None] * jnp.einsum(
        "chpn,ctn->cthp", entering, queries, precision=PRECISE
    )
    mixed_out = (intra_out + inter_out + skip[None, None, :, None] * inputs).reshape(
        token_count, channels
    )
    mixer = (mixed_out * jax.nn.silu(z_gate.astype(jnp.float32))).astype(jnp.bfloat16)
    token_mix = lax.all_to_all(mixer, "exp", split_axis=0, concat_axis=1, tiled=True)
    stream = (residual.astype(jnp.float32) + token_mix.astype(jnp.float32)).astype(jnp.bfloat16)
    widened = stream.astype(jnp.float32)
    normed = (
        widened
        * lax.rsqrt(jnp.mean(widened * widened, axis=-1, keepdims=True) + 1e-06)
        * norm_gain[None, :]
    ).astype(jnp.bfloat16)
    rows_here = residual.shape[0]
    owners = lax.axis_size("exp")
    local_experts = w_gate.shape[0]
    experts = owners * local_experts
    capacity = max(2, 2 * rows_here // experts + 1)
    width = residual.shape[1]
    chosen = expert_ids.reshape(-1)
    onehot = (chosen[:, None] == jnp.arange(experts)[None, :]).astype(jnp.int32)
    slot_index = jnp.sum((jnp.cumsum(onehot, axis=0) - onehot) * onehot, axis=1)
    target = chosen * capacity + slot_index
    placing = (target[None, :] == jnp.arange(experts * capacity)[:, None]).astype(jnp.bfloat16)
    pair_rows = jnp.repeat(normed, 2, axis=0)
    outgoing = jnp.dot(placing, pair_rows, preferred_element_type=jnp.float32).astype(jnp.bfloat16)
    outgoing = outgoing.reshape(owners, local_experts, 1, capacity, width)
    arrived = lax.all_to_all(outgoing, "exp", split_axis=0, concat_axis=2, tiled=True)
    segment = lax.all_gather(arrived, "seq", axis=1, tiled=True)
    flattened = segment.reshape(segment.shape[0], -1, segment.shape[-1])
    gate_proj = jnp.einsum("erd,edf->erf", flattened, w_gate, preferred_element_type=jnp.float32)
    up_proj = jnp.einsum("erd,edf->erf", flattened, w_up, preferred_element_type=jnp.float32)
    active = (jax.nn.silu(gate_proj) * up_proj).astype(jnp.bfloat16)
    partial_value = jnp.einsum("erf,efd->erd", active, w_down, preferred_element_type=jnp.float32)
    partials = partial_value.reshape(segment.shape[:-1] + (partial_value.shape[-1],))
    summed = lax.psum_scatter(partials.astype(jnp.bfloat16), "seq", scatter_dimension=1, tiled=True)
    returned = lax.all_to_all(summed, "exp", split_axis=2, concat_axis=0, tiled=True)
    results = returned.reshape(experts * capacity, width)
    picked = results[target].astype(jnp.float32).reshape(rows_here, 2, width)
    mixture = jnp.sum(picked * gate_weights[:, :, None], axis=1)
    return (widened + mixture).astype(jnp.bfloat16)


def solution(mesh):
    return jax.shard_map(
        on_device,
        mesh=mesh,
        in_specs=(
            P("seq", "exp"),
            P("seq", "exp"),
            P("seq", None),
            P("seq", None),
            P("seq", "exp"),
            P("exp"),
            P("exp"),
            P("exp", None, None),
            P(("seq", "exp"), None),
            P(),
            P(("seq", "exp"), None),
            P(("seq", "exp"), None),
            P("exp", None, "seq"),
            P("exp", None, "seq"),
            P("exp", "seq", None),
        ),
        out_specs=P(("seq", "exp"), None),
        check_vma=False,
    )
```

profile of v0, /device:TPU:1, one launch (start us, length us, event | category | flops | bytes accessed | tf_op | source)
XLA Modules:
  0.0 454.0 jit_solution(192723632810441709)
XLA Ops:
  8.6 1.3 reshape.209
  10.6 4.3 while.33
  11.5 1.3 dynamic_update_slice.14
  13.6 1.3 dynamic_update_slice.14
  16.3 1.3 dynamic-slice
  18.5 34.4 %all-reduce = bf16[128]{0:T(256)(128)(2,1)S(1)} all-reduce(bf16[128]{0:T(256)(128)(2,1)S(1)} %dynamic-update-slice), channel_id=2, replica_groups=mesh['seq'=16,'exp'=16] {'seq'}, use_global_device_ids=true, to_apply=%add | all-reduce | flops 128 | bytes 512
  53.7 1.1 copy.84
  55.2 13.5 %all-gather.6.cloned.1.call-done = bf16[128,64,128]{2,1,0:T(8,128)(2,1)} async-done(((bf16[8,64,128]{2,1,0:T(8,128)(2,1)}), bf16[128,64,128]{2,1,0:T(8,128)(2,1)}) %all-gather.6.cloned.1.call-update) | async-done | bytes 2097168 | tf_op jit(solution)/shard_map/all_gather | solution.py:13
  68.7 17.0 %while.34 = (s32[]{:T(128)}, f32[8]{0:T(128)S(1)}, f32[8,64,128]{2,1,0:T(8,128)S(1)}, s32[]{:T(128)}, bf16[16,8]{1,0:T(8,128)(2,1)S(1)}, /*index=5*/bf16[16,8,64,128]{3,2,1,0:T(8,128)(2,1)}, s32[]{:T(128)}, s32[]{:T(128)}) while((s32[]{:T(128)}, f32[8]{0:T(128)S(1)}, f32[8,64,128]{2,1,0:T(8,128)S(1)}, s32[]{:T(128)}, ...), condition=%wide.region_4.5_spmd.clone, body=%wide.region_3.4_spmd.clone.sunk | while | flops 327716 | bytes 655619 | solution.py:30
  85.7 1.0 multiply_add_fusion
  86.7 1.5 fusion.13
  88.2 1.3 fusion.12
  91.0 8.5 %all-to-all-start = ((bf16[16,16,512]{2,1,0:T(8,128)(2,1)}), bf16[16,16,512]{2,1,0:T(8,128)(2,1)S(1)}, u32[]{:S(2)}, u32[]{:S(2)}) async-start(bf16[16,16,512]{2,1,0:T(8,128)(2,1)} %bitcast.12), calls=%async_computation | async-start | bytes 524288 | tf_op jit(solution)/shard_map/all_to_all | solution.py:99
  99.9 11.3 %all-to-all-done = bf16[16,16,512]{2,1,0:T(8,128)(2,1)S(1)} async-done(((bf16[16,16,512]{2,1,0:T(8,128)(2,1)}), bf16[16,16,512]{2,1,0:T(8,128)(2,1)S(1)}, u32[]{:S(2)}, u32[]{:S(2)}) %all-to-all-start) | async-done | bytes 262176 | tf_op jit(solution)/shard_map/all_to_all | solution.py:99
  112.4 1.2 convolution_convert_fusion.1
  113.6 1.5 reshape.174
  115.1 31.2 %all_to_all.34 = bf16[16,1,1,3,8192]{4,3,2,1,0:T(4,128)(2,1)S(1)} all-to-all(bf16[16,1,1,3,8192]{4,3,2,1,0:T(4,128)(2,1)S(1)} %bitcast.114), channel_id=1, replica_groups=mesh['seq'=16,'exp'=16] {'exp'}, dimensions={0} | all-to-all | bytes 1572864 | tf_op jit(solution)/shard_map/all_to_all | solution.py:121
  146.3 1.5 copy.89
  148.0 89.6 %all-gather.8.cloned.1.call-done = bf16[256,1,1,3,8192]{4,0,3,2,1:T(8,128)(2,1)} async-done(((bf16[16,1,1,3,8192]{4,0,3,2,1:T(8,128)(2,1)}), bf16[256,1,1,3,8192]{4,0,3,2,1:T(8,128)(2,1)}) %all-gather.8.cloned.1.call-update) | async-done | bytes 12582928 | tf_op jit(solution)/shard_map/all_gather | solution.py:122
  237.6 18.8 %copy.90 = bf16[256,1,1,3,8192]{4,3,0,2,1:T(4,128)(2,1)} copy(bf16[256,1,1,3,8192]{4,0,3,2,1:T(8,128)(2,1)} %all-gather.8.cloned.1.call-done) | data formatting | bytes 25165824 | tf_op jit(solution)/shard_map/all_gather | solution.py:122
  256.4 26.2 %reshape.175 = bf16[768,8192]{1,0:T(8,128)(2,1)} reshape(bf16[256,1,1,3,8192]{4,3,0,2,1:T(4,128)(2,1)} %copy.90) | data formatting | bytes 25165824 | tf_op jit(solution)/shard_map/reshape.2
  282.7 7.7 %fusion.9 = f32[768,128]{1,0:T(8,128)S(1)} fusion(bf16[768,8192]{1,0:T(8,128)(2,1)} %reshape.175, bf16[1,8192,128]{2,1,0:T(8,128)(2,1)} %param.31), kind=kOutput, calls=%fused_computation.21 | convolution fusion | flops 1610612736 | bytes 15073280 | tf_op jit(solution)/shard_map/erd,edf->erf/dot_general | solution.py:124
  292.0 3.4 fusion.17
  295.6 6.4 %fusion.5 = bf16[1,16,16,3,8192]{4,2,3,1,0:T(8,128)(2,1)} fusion(bf16[1,128,8192]{2,1,0:T(8,128)(2,1)S(1)} %copy-done, bf16[16,16,3,128]{3,2,1,0:T(4,128)(2,1)S(1)} %dot_general.46), kind=kOutput, calls=%fused_computation.16 | convolution fusion | flops 1616904192 | bytes 14876672 | tf_op jit(solution)/shard_map/erf,efd->erd/dot_general | solution.py:127
  302.0 99.5 %reduce-scatter.7.cloned.1.call-done = bf16[1,1,16,3,8192]{4,2,3,1,0:T(8,128)(2,1)} async-done(((bf16[1,16,16,3,8192]{4,2,3,1,0:T(8,128)(2,1)}), bf16[1,1,16,3,8192]{4,2,3,1,0:T(8,128)(2,1)}) %reduce-scatter.7.cloned.1.call-update) | async-done | bytes 786448
  401.5 2.8 copy.92
  404.2 7.9 %all-to-all-start.2 = ((bf16[1,1,16,3,8192]{4,3,1,0,2:T(4,128)(2,1)}), bf16[1,1,16,3,8192]{4,3,1,0,2:T(4,128)(2,1)}, u32[]{:S(2)}, u32[]{:S(2)}) async-start(bf16[1,1,16,3,8192]{4,3,1,0,2:T(4,128)(2,1)} %copy.92), calls=%async_computation.2 | async-start | bytes 2097152 | tf_op jit(solution)/shard_map/all_to_all | solution.py:130
  412.4 27.8 %all-to-all-done.2 = bf16[1,1,16,3,8192]{4,3,1,0,2:T(4,128)(2,1)} async-done(((bf16[1,1,16,3,8192]{4,3,1,0,2:T(4,128)(2,1)}), bf16[1,1,16,3,8192]{4,3,1,0,2:T(4,128)(2,1)}, u32[]{:S(2)}, u32[]{:S(2)}) %all-to-all-start.2) | async-done | bytes 786464 | tf_op jit(solution)/shard_map/all_to_all | solution.py:130
  440.2 1.7 reshape.179
  441.9 1.7 gather_fusion
  443.6 1.7 reshape.183
  445.3 1.4 multiply_reduce_fusion
  (116 shorter events, 29.6 us)
Async XLA Ops:
  6.5 289.0 %copy-start = (bf16[1,128,8192]{2,1,0:T(8,128)(2,1)S(1)}, bf16[1,128,8192]{2,1,0:T(8,128)(2,1)}, u32[]{:S(2)}) copy-start(bf16[1,128,8192]{2,1,0:T(8,128)(2,1)} %param.33) | copy-start | bytes 6291460
  6.5 3.7 copy-start.4
  6.5 62.1 %all-gather.6.cloned.1.call-start = ((), (), s32[]{:S(2)}) async-start(), calls=%async_computation.4 | async-start | bytes 2228224 | tf_op jit(solution)/shard_map/all_gather | solution.py:13
  10.6 44.2 %copy-start.7 = (s32[16,2]{0,1:T(2,128)S(1)}, s32[16,2]{0,1:T(2,128)}, u32[]{:S(2)}) copy-start(s32[16,2]{0,1:T(2,128)} %param.29) | copy-start | bytes 388
  10.6 44.4 %copy-start.2 = (bf16[256,128]{1,0:T(8,128)(2,1)S(1)}, bf16[256,128]{1,0:T(8,128)(2,1)}, u32[]{:S(2)}) copy-start(bf16[256,128]{1,0:T(8,128)(2,1)} %param.22) | copy-start | bytes 196612
  68.7 19.5 %copy-start.6 = (f32[2,128,8]{1,2,0:T(8,128)S(1)}, f32[2,128,8]{1,2,0:T(8,128)}, u32[]{:S(2)}) copy-start(f32[2,128,8]{1,2,0:T(8,128)} %copy.76) | copy-start | bytes 24580
  68.7 19.5 %copy-start.10 = (f32[8]{0:T(128)S(1)}, f32[8]{0:T(128)}, u32[]{:S(2)}) copy-start(f32[8]{0:T(128)} %param.25) | copy-start | bytes 100
  90.0 21.4 %copy-start.3 = (bf16[16,8192]{1,0:T(8,128)(2,1)S(1)}, bf16[16,8192]{1,0:T(8,128)(2,1)}, u32[]{:S(2)}) copy-start(bf16[16,8192]{1,0:T(8,128)(2,1)} %param.27) | copy-start | bytes 786436
  90.2 21.4 %copy-start.5 = (f32[8192]{0:T(1024)S(1)}, f32[8192]{0:T(1024)}, u32[]{:S(2)}) copy-start(f32[8192]{0:T(1024)} %param.28) | copy-start | bytes 98308
  91.0 20.2 %all-to-all-start = ((bf16[16,16,512]{2,1,0:T(8,128)(2,1)}), bf16[16,16,512]{2,1,0:T(8,128)(2,1)S(1)}, u32[]{:S(2)}, u32[]{:S(2)}) async-start(bf16[16,16,512]{2,1,0:T(8,128)(2,1)} %bitcast.12), calls=%async_computation | async-start | bytes 524288 | tf_op jit(solution)/shard_map/all_to_all | solution.py:99
  99.6 138.0 %all-gather.8.cloned.1.call-start = ((), (), s32[]{:S(2)}) async-start(), calls=%async_computation.5 | async-start | bytes 13369344 | tf_op jit(solution)/shard_map/all_gather | solution.py:122
  147.8 253.7 %reduce-scatter.7.cloned.1.call-start = ((), (), s32[]{:S(2)}) async-start(), calls=%async_computation.6 | async-start | bytes 13369344
  282.7 8.8 %copy-start.1 = (bf16[768,8192]{1,0:T(8,128)(2,1)S(1)}, bf16[768,8192]{1,0:T(8,128)(2,1)}, u32[]{:S(2)}) copy-start(bf16[768,8192]{1,0:T(8,128)(2,1)} %reshape.175) | copy-start | bytes 37748740
  282.7 9.4 %copy-start.9 = (bf16[1,8192,128]{2,1,0:T(8,128)(2,1)S(1)}, bf16[1,8192,128]{2,1,0:T(8,128)(2,1)}, u32[]{:S(2)}) copy-start(bf16[1,8192,128]{2,1,0:T(8,128)(2,1)} %param.32) | copy-start | bytes 6291460
  302.0 110.4 %copy-start.8 = (f32[16,2]{0,1:T(2,128)S(1)}, f32[16,2]{0,1:T(2,128)}, u32[]{:S(2)}) copy-start(f32[16,2]{0,1:T(2,128)} %param.30) | copy-start | bytes 388
  404.2 35.9 %all-to-all-start.2 = ((bf16[1,1,16,3,8192]{4,3,1,0,2:T(4,128)(2,1)}), bf16[1,1,16,3,8192]{4,3,1,0,2:T(4,128)(2,1)}, u32[]{:S(2)}, u32[]{:S(2)}) async-start(bf16[1,1,16,3,8192]{4,3,1,0,2:T(4,128)(2,1)} %copy.92), calls=%async_computation.2 | async-start | bytes 2097152 | tf_op jit(solution)/shard_map/all_to_all | solution.py:130
Sparse Core Ops, SparseCore 0:
  15.7 52.9 all-gather.5
  147.9 89.6 all-gather.7
  302.1 99.3 reduce-scatter.6
where the time goes:
time: 456 us; the launch traced here: 454 us
  waiting for transfers between devices  242 us (53%)
  local copies, waits for them, and re-layouts  68.5 us (15%)
  blocking collectives  65.6 us (14%)
  other arithmetic  24.9 us (5%)
  matrix products  22.1 us (5%)
  starting transfers between devices  16.7 us (4%)
  between operations  14.1 us (3%)
    unnamed x4, waiting for transfers between devices  99.5 us
    all_gather x1, waiting for transfers between devices, on_device(): segment = lax.all_gather(arrived, 'seq', axis=1, tiled=True)  89.6 us
    unnamed x1, blocking collectives  34.4 us
    all_to_all x1, blocking collectives, on_device(): lax.all_to_all(outgoing, 'exp', split_axis=0, concat_axis=2, tiled=True)  31.2 us
    all_to_all x1, waiting for transfers between devices, on_device(): lax.all_to_all(summed, 'exp', split_axis=2, concat_axis=0, tiled=True)  27.8 us
    another operation x1, local copies, waits for them, and re-layouts  26.2 us
    all_gather x1, local copies, waits for them, and re-layouts, on_device(): segment = lax.all_gather(arrived, 'seq', axis=1, tiled=True)  18.8 us
    select_n x16, other arithmetic, hop(): return jax.tree.map(lambda a, b: jnp.where(reached, a, b), new, before)  16.2 us
  transfers between devices with their start and end apart: 5, of which 5 were waited for; matrix products, arithmetic and copies ran while one was open for 1% of the time, Pallas kernels for 0%

commit v1 on v0

--- a/solution.py
+++ b/solution.py
@@ -119,7 +119,9 @@
     outgoing = jnp.dot(placing, pair_rows, preferred_element_type=jnp.float32).astype(jnp.bfloat16)
     outgoing = outgoing.reshape(owners, local_experts, 1, capacity, width)
     arrived = lax.all_to_all(outgoing, "exp", split_axis=0, concat_axis=2, tiled=True)
-    segment = lax.all_gather(arrived, "seq", axis=1, tiled=True)
+    segment = jnp.concatenate(
+        lax.all_to_all(jnp.stack([arrived] * lax.axis_size("seq")), "seq", 0, 0), axis=1
+    )
     flattened = segment.reshape(segment.shape[0], -1, segment.shape[-1])
     gate_proj = jnp.einsum("erd,edf->erf", flattened, w_gate, preferred_element_type=jnp.float32)
     up_proj = jnp.einsum("erd,edf->erf", flattened, w_up, preferred_element_type=jnp.float32)

time: 456 us -> 504 us (1.11)
  blocking collectives: 65.6 us -> 212 us
  waiting for transfers between devices: 242 us -> 145 us
    all_to_all x0 -> x1, blocking collectives: none -> 146 us  [on_device(): lax.all_to_all(jnp.stack([arrived] * lax.axis_size('seq')), 'seq', 0, 0)]
    all_gather x1 -> x0, waiting for transfers between devices: 89.6 us -> none  [on_device(): segment = lax.all_gather(arrived, 'seq', axis=1, tiled=True)]
    all_gather x1 -> x0, local copies, waits for them, and re-layouts: 18.8 us -> none  [on_device(): segment = lax.all_gather(arrived, 'seq', axis=1, tiled=True)]
    all_to_all x1, local copies, waits for them, and re-layouts: 1.46 us -> 12.1 us  [on_device(): lax.all_to_all(jnp.stack([arrived] * lax.axis_size('seq')), 'seq', 0, 0)]
    unnamed x4 -> x3, waiting for transfers between devices: 99.5 us -> 92.2 us
    another operation x1 -> x3, local copies, waits for them, and re-layouts: 26.2 us -> 33 us
  transfers between devices with their start and end apart: 5 -> 4, of which waited for: 5 -> 4; matrix products, arithmetic and copies ran while one was open for 1% -> 1% of each run, Pallas kernels for 0% -> 0%
where the time goes in v1:
time: 504 us; the launch traced here: 502 us
  blocking collectives  212 us (42%)
  waiting for transfers between devices  145 us (29%)
  local copies, waits for them, and re-layouts  67 us (13%)
  other arithmetic  24.9 us (5%)
  matrix products  22 us (4%)
  starting transfers between devices  16.5 us (3%)
  between operations  14.4 us (3%)
    all_to_all x1, blocking collectives, on_device(): lax.all_to_all(jnp.stack([arrived] * lax.axis_size('seq')), 'seq', 0, 0)  146 us
    unnamed x3, waiting for transfers between devices  92.2 us
    unnamed x1, blocking collectives  34.3 us
    all_to_all x1, blocking collectives, on_device(): lax.all_to_all(outgoing, 'exp', split_axis=0, concat_axis=2, tiled=True)  31.2 us
    all_to_all x1, waiting for transfers between devices, on_device(): lax.all_to_all(summed, 'exp', split_axis=2, concat_axis=0, tiled=True)  27.8 us
    another operation x1, local copies, waits for them, and re-layouts  26.3 us
    select_n x16, other arithmetic, hop(): return jax.tree.map(lambda a, b: jnp.where(reached, a, b), new, before)  16.2 us
    all_gather x1, waiting for transfers between devices, entering_2(): lax.all_gather(part.astype(kind), axis)  13.6 us
  transfers between devices with their start and end apart: 4, of which 4 were waited for; matrix products, arithmetic and copies ran while one was open for 1% of the time, Pallas kernels for 0%

profile of v1, /device:TPU:1, one launch (start us, length us, event | category | flops | bytes accessed | tf_op | source)
XLA Modules:
  0.0 501.9 jit_solution(8072472494756127829)
XLA Ops:
  8.6 1.3 reshape.211
  10.6 4.2 while.33
  11.5 1.3 dynamic_update_slice.14
  13.6 1.3 dynamic_update_slice.14
  16.3 1.3 dynamic-slice
  18.4 34.3 %all-reduce = bf16[128]{0:T(256)(128)(2,1)S(1)} all-reduce(bf16[128]{0:T(256)(128)(2,1)S(1)} %dynamic-update-slice), channel_id=2, replica_groups=mesh['seq'=16,'exp'=16] {'seq'}, use_global_device_ids=true, to_apply=%add | all-reduce | flops 128 | bytes 512
  53.5 1.1 copy.84
  55.0 13.6 %all-gather.4.cloned.1.call-done = bf16[128,64,128]{2,1,0:T(8,128)(2,1)} async-done(((bf16[8,64,128]{2,1,0:T(8,128)(2,1)}), bf16[128,64,128]{2,1,0:T(8,128)(2,1)}) %all-gather.4.cloned.1.call-update) | async-done | bytes 2097168 | tf_op jit(solution)/shard_map/all_gather | solution.py:13
  68.7 17.0 %while.34 = (s32[]{:T(128)}, f32[8]{0:T(128)S(1)}, f32[8,64,128]{2,1,0:T(8,128)S(1)}, s32[]{:T(128)}, bf16[16,8]{1,0:T(8,128)(2,1)S(1)}, /*index=5*/bf16[16,8,64,128]{3,2,1,0:T(8,128)(2,1)}, s32[]{:T(128)}, s32[]{:T(128)}) while((s32[]{:T(128)}, f32[8]{0:T(128)S(1)}, f32[8,64,128]{2,1,0:T(8,128)S(1)}, s32[]{:T(128)}, ...), condition=%wide.region_4.5_spmd.clone, body=%wide.region_3.4_spmd.clone.sunk | while | flops 327716 | bytes 655619 | solution.py:30
  86.7 1.5 fusion.13
  88.2 1.3 fusion.12
  91.0 8.5 %all-to-all-start = ((bf16[16,16,512]{2,1,0:T(8,128)(2,1)}), bf16[16,16,512]{2,1,0:T(8,128)(2,1)S(1)}, u32[]{:S(2)}, u32[]{:S(2)}) async-start(bf16[16,16,512]{2,1,0:T(8,128)(2,1)} %bitcast.12), calls=%async_computation | async-start | bytes 524288 | tf_op jit(solution)/shard_map/all_to_all | solution.py:99
  99.9 11.3 %all-to-all-done = bf16[16,16,512]{2,1,0:T(8,128)(2,1)S(1)} async-done(((bf16[16,16,512]{2,1,0:T(8,128)(2,1)}), bf16[16,16,512]{2,1,0:T(8,128)(2,1)S(1)}, u32[]{:S(2)}, u32[]{:S(2)}) %all-to-all-start) | async-done | bytes 262176 | tf_op jit(solution)/shard_map/all_to_all | solution.py:99
  112.3 1.2 convolution_convert_fusion.1
  113.6 1.5 reshape.178
  115.0 31.2 %all_to_all.36 = bf16[16,1,1,3,8192]{4,3,2,1,0:T(4,128)(2,1)S(1)} all-to-all(bf16[16,1,1,3,8192]{4,3,2,1,0:T(4,128)(2,1)S(1)} %bitcast.115), channel_id=1, replica_groups=mesh['seq'=16,'exp'=16] {'exp'}, dimensions={0} | all-to-all | bytes 1572864 | tf_op jit(solution)/shard_map/all_to_all | solution.py:121
  146.9 6.1 %stack.5 = bf16[16,1,1,16,3,8192]{5,3,4,2,1,0:T(8,128)(2,1)} broadcast(bf16[16,3,8192]{2,0,1:T(8,128)(2,1)S(1)} %copy.89), dimensions={3,4,5} | broadcast | bytes 13369344 | tf_op jit(solution)/shard_map/stack | solution.py:123
  153.0 146.2 %all_to_all.37 = bf16[16,1,1,16,3,8192]{5,3,4,2,1,0:T(8,128)(2,1)S(1)} all-to-all(bf16[16,1,1,16,3,8192]{5,3,4,2,1,0:T(8,128)(2,1)} %stack.5), channel_id=1, replica_groups=mesh['seq'=16,'exp'=16] {'seq'}, dimensions={0} | all-to-all | bytes 25165824 | tf_op jit(solution)/shard_map/all_to_all | solution.py:123
  299.2 12.1 %copy.90 = bf16[16,1,1,16,3,8192]{5,4,3,0,2,1:T(4,128)(2,1)} copy(bf16[16,1,1,16,3,8192]{5,3,4,2,1,0:T(8,128)(2,1)S(1)} %all_to_all.37) | data formatting | bytes 25165824 | tf_op jit(solution)/shard_map/all_to_all | solution.py:123
  311.3 26.3 %reshape.179 = bf16[768,8192]{1,0:T(8,128)(2,1)} reshape(bf16[16,1,1,16,3,8192]{5,4,3,0,2,1:T(4,128)(2,1)} %copy.90) | data formatting | bytes 25165824 | tf_op jit(solution)/shard_map/reshape.4
  337.6 7.7 %fusion.9 = f32[768,128]{1,0:T(8,128)S(1)} fusion(bf16[768,8192]{1,0:T(8,128)(2,1)} %reshape.179, bf16[1,8192,128]{2,1,0:T(8,128)(2,1)} %param.31), kind=kOutput, calls=%fused_computation.21 | convolution fusion | flops 1610612736 | bytes 15073280 | tf_op jit(solution)/shard_map/erd,edf->erf/dot_general | solution.py:126
  345.3 1.1 copy-done.1
  347.0 3.4 fusion.17
  350.5 6.3 %fusion.5 = bf16[1,16,16,3,8192]{4,2,3,1,0:T(8,128)(2,1)} fusion(bf16[1,128,8192]{2,1,0:T(8,128)(2,1)S(1)} %copy-done, bf16[16,16,3,128]{3,2,1,0:T(4,128)(2,1)S(1)} %dot_general.46), kind=kOutput, calls=%fused_computation.16 | convolution fusion | flops 1616904192 | bytes 14876672 | tf_op jit(solution)/shard_map/erf,efd->erd/dot_general | solution.py:129
  356.9 92.1 %reduce-scatter.7.cloned.1.call-done = bf16[1,1,16,3,8192]{4,2,3,1,0:T(8,128)(2,1)} async-done(((bf16[1,16,16,3,8192]{4,2,3,1,0:T(8,128)(2,1)}), bf16[1,1,16,3,8192]{4,2,3,1,0:T(8,128)(2,1)}) %reduce-scatter.7.cloned.1.call-update) | async-done | bytes 786448
  449.0 2.8 copy.92
  451.8 7.9 %all-to-all-start.3 = ((bf16[1,1,16,3,8192]{4,3,1,0,2:T(4,128)(2,1)}), bf16[1,1,16,3,8192]{4,3,1,0,2:T(4,128)(2,1)}, u32[]{:S(2)}, u32[]{:S(2)}) async-start(bf16[1,1,16,3,8192]{4,3,1,0,2:T(4,128)(2,1)} %copy.92), calls=%async_computation.3 | async-start | bytes 2097152 | tf_op jit(solution)/shard_map/all_to_all | solution.py:132
  460.0 27.8 %all-to-all-done.3 = bf16[1,1,16,3,8192]{4,3,1,0,2:T(4,128)(2,1)} async-done(((bf16[1,1,16,3,8192]{4,3,1,0,2:T(4,128)(2,1)}), bf16[1,1,16,3,8192]{4,3,1,0,2:T(4,128)(2,1)}, u32[]{:S(2)}, u32[]{:S(2)}) %all-to-all-start.3) | async-done | bytes 786464 | tf_op jit(solution)/shard_map/all_to_all | solution.py:132
  487.7 1.7 reshape.183
  489.5 1.7 gather_fusion
  491.1 1.7 reshape.187
  492.8 1.4 multiply_reduce_fusion
  (115 shorter events, 30.0 us)
Async XLA Ops:
  6.5 344.0 %copy-start = (bf16[1,128,8192]{2,1,0:T(8,128)(2,1)S(1)}, bf16[1,128,8192]{2,1,0:T(8,128)(2,1)}, u32[]{:S(2)}) copy-start(bf16[1,128,8192]{2,1,0:T(8,128)(2,1)} %param.33) | copy-start | bytes 6291460
  6.5 3.7 copy-start.4
  6.5 62.1 %all-gather.4.cloned.1.call-start = ((), (), s32[]{:S(2)}) async-start(), calls=%async_computation.5 | async-start | bytes 2228224 | tf_op jit(solution)/shard_map/all_gather | solution.py:13
  10.6 44.0 %copy-start.7 = (s32[16,2]{0,1:T(2,128)S(1)}, s32[16,2]{0,1:T(2,128)}, u32[]{:S(2)}) copy-start(s32[16,2]{0,1:T(2,128)} %param.29) | copy-start | bytes 388
  10.6 44.2 %copy-start.2 = (bf16[256,128]{1,0:T(8,128)(2,1)S(1)}, bf16[256,128]{1,0:T(8,128)(2,1)}, u32[]{:S(2)}) copy-start(bf16[256,128]{1,0:T(8,128)(2,1)} %param.22) | copy-start | bytes 196612
  68.7 19.5 %copy-start.6 = (f32[2,128,8]{1,2,0:T(8,128)S(1)}, f32[2,128,8]{1,2,0:T(8,128)}, u32[]{:S(2)}) copy-start(f32[2,128,8]{1,2,0:T(8,128)} %copy.76) | copy-start | bytes 24580
  68.7 19.5 %copy-start.10 = (f32[8]{0:T(128)S(1)}, f32[8]{0:T(128)}, u32[]{:S(2)}) copy-start(f32[8]{0:T(128)} %param.25) | copy-start | bytes 100
  90.0 21.4 %copy-start.3 = (bf16[16,8192]{1,0:T(8,128)(2,1)S(1)}, bf16[16,8192]{1,0:T(8,128)(2,1)}, u32[]{:S(2)}) copy-start(bf16[16,8192]{1,0:T(8,128)(2,1)} %param.27) | copy-start | bytes 786436
  90.1 21.4 %copy-start.5 = (f32[8192]{0:T(1024)S(1)}, f32[8192]{0:T(1024)}, u32[]{:S(2)}) copy-start(f32[8192]{0:T(1024)} %param.28) | copy-start | bytes 98308
  91.0 20.2 %all-to-all-start = ((bf16[16,16,512]{2,1,0:T(8,128)(2,1)}), bf16[16,16,512]{2,1,0:T(8,128)(2,1)S(1)}, u32[]{:S(2)}, u32[]{:S(2)}) async-start(bf16[16,16,512]{2,1,0:T(8,128)(2,1)} %bitcast.12), calls=%async_computation | async-start | bytes 524288 | tf_op jit(solution)/shard_map/all_to_all | solution.py:99
  99.5 349.5 %reduce-scatter.7.cloned.1.call-start = ((), (), s32[]{:S(2)}) async-start(), calls=%async_computation.6 | async-start | bytes 13369344
  337.6 8.8 %copy-start.1 = (bf16[768,8192]{1,0:T(8,128)(2,1)S(1)}, bf16[768,8192]{1,0:T(8,128)(2,1)}, u32[]{:S(2)}) copy-start(bf16[768,8192]{1,0:T(8,128)(2,1)} %reshape.179) | copy-start | bytes 37748740
  337.6 9.4 %copy-start.9 = (bf16[1,8192,128]{2,1,0:T(8,128)(2,1)S(1)}, bf16[1,8192,128]{2,1,0:T(8,128)(2,1)}, u32[]{:S(2)}) copy-start(bf16[1,8192,128]{2,1,0:T(8,128)(2,1)} %param.32) | copy-start | bytes 6291460
  356.9 103.0 %copy-start.8 = (f32[16,2]{0,1:T(2,128)S(1)}, f32[16,2]{0,1:T(2,128)}, u32[]{:S(2)}) copy-start(f32[16,2]{0,1:T(2,128)} %param.30) | copy-start | bytes 388
  451.8 35.9 %all-to-all-start.3 = ((bf16[1,1,16,3,8192]{4,3,1,0,2:T(4,128)(2,1)}), bf16[1,1,16,3,8192]{4,3,1,0,2:T(4,128)(2,1)}, u32[]{:S(2)}, u32[]{:S(2)}) async-start(bf16[1,1,16,3,8192]{4,3,1,0,2:T(4,128)(2,1)} %copy.92), calls=%async_computation.3 | async-start | bytes 2097152 | tf_op jit(solution)/shard_map/all_to_all | solution.py:132
Sparse Core Ops, SparseCore 0:
  15.7 52.9 all-gather.3
  357.0 91.9 reduce-scatter.6
